TPU v7x, 32 devices: a whole 2x2x4 slice. The times are simulated.
32 devices in a mesh: src: 8 (over y, x, core), dst: 4 (over z).
Axes of the slice: x: 2, y: 2, z: 4, core: 2. Of those that a mesh axis runs over, the one named last changes fastest.
Arguments:
- raw: bfloat16 [4096, 256], P(('src', 'dst')), may hold values from -6 to 6
- enc_w1: bfloat16 [256, 512], replicated, may hold values from -0.375 to 0.375
- enc_w2: bfloat16 [512, 256], replicated, may hold values from -0.25 to 0.25
- block_weights: float32 [512, 128, 128], P(('src', 'dst')), may hold values from -0.125 to 0.125
- block_cols: int32 [512], P(('src', 'dst')), may hold values from 0 to 3, as said below
- noise: bfloat16 [3, 4096, 256], P(None, ('src', 'dst')), may hold values from -3 to 3
Outputs:
- encoded: bfloat16 [4096, 256], P(('src', 'dst'))
- hops: bfloat16 [3, 4096, 256], P(None, ('src', 'dst'))
Inputs may be any that keep to these rules, and one draw needn't show every extreme that they name: `block_cols`: entry b of each device's 16 entries belongs to row block b // 2; row blocks 2j and 2j+1 of a device together name every column block exactly once, each naming 4 // 2 distinct ones.
All inputs are finite; a program needn't handle non-finite values.
Results may differ from a plain program's by a relative error of at most 0.0058.
Values may be sent and summed in bfloat16 or wider, within the bound.
A program may use at most 128 MiB of HBM per device.

v0:
```python
import jax
import jax.numpy as jnp
from jax import lax
from jax.sharding import PartitionSpec as P

HOPS = 3


def normalize_rows(z):
    return (z * lax.rsqrt(jnp.mean(z * z, axis=-1, keepdims=True) + 1e-06)).astype(jnp.bfloat16)


def shards(raw, enc_w1, enc_w2, block_weights, block_cols, noise):
    hidden = jax.nn.silu(jnp.dot(raw, enc_w1, preferred_element_type=jnp.float32)).astype(
        jnp.bfloat16
    )
    encoded = normalize_rows(jnp.dot(hidden, enc_w2, preferred_element_type=jnp.float32))
    own_rows = raw.shape[0]
    block_side = block_weights.shape[1]
    width = encoded.shape[1]
    feats = encoded
    kept = []
    for step in range(HOPS):
        group = lax.all_gather(feats, "dst", axis=0, tiled=True)
        col_count = group.shape[0] // block_side
        half = col_count // 2
        col_blocks = group.astype(jnp.float32).reshape(col_count, block_side, width)
        fetched = jnp.take(col_blocks, block_cols, axis=0)
        prods = jnp.einsum("bij,bjw->biw", block_weights, fetched, precision=lax.Precision.HIGHEST)
        mine = lax.psum_scatter(
            prods.reshape(own_rows * lax.axis_size("src") // block_side, half, block_side, width)
            .sum(axis=1)
            .reshape(own_rows * lax.axis_size("src"), width),
            "src",
            scatter_dimension=0,
            tiled=True,
        )
        feats = normalize_rows(mine + noise[step].astype(jnp.float32))
        kept.append(feats)
    return (encoded, jnp.stack(kept))


def solution(mesh):
    placed = (
        P(("src", "dst"), None),
        P(),
        P(),
        P(("src", "dst"), None, None),
        P(("src", "dst")),
        P(None, ("src", "dst"), None),
    )
    return jax.shard_map(
        shards,
        mesh=mesh,
        in_specs=placed,
        out_specs=(P(("src", "dst"), None), P(None, ("src", "dst"), None)),
        check_vma=False,
    )
```

profile of v0, /device:TPU:0, one launch (start us, length us, event | category | flops | bytes accessed | tf_op | source)
XLA Modules:
  0.0 204.7 jit_solution(9608763618662152512)
XLA Ops:
  7.2 0.0 reduce-scatter.4.cloned.1.call-start
  7.2 0.7 compare_and_fusion
  8.0 0.7 compare_select_fusion
  8.6 1.5 multiply_reduce_fusion.3
  10.1 0.1 multiply_convert_fusion.4
  10.2 15.7 %all_gather.9 = bf16[512,256]{1,0:T(8,128)(2,1)S(1)} all-gather(bf16[128,256]{1,0:T(8,128)(2,1)S(1)} %multiply_convert_fusion.4), channel_id=1, replica_groups=mesh['src'=8,'dst'=4] {'dst'}, dimensions={0}, use_global_device_ids=true | all-gather | bytes 327680 | tf_op jit(solution)/shard_map/all_gather | solution.py:24
  25.9 2.0 gather_fusion
  28.0 5.4 %bitcast_reduce_fusion.2 = f32[8,128,256]{1,2,0:T(8,128)S(1)} fusion(f32[16,128,128]{2,1,0:T(8,128)S(1)} %copy-done, f32[16,128,256]{2,1,0:T(8,128)} %gather_fusion, pred[16]{0:T(512)(128)(4,1)S(1)} %compare_and_fusion), kind=kOutput, calls=%fused_computation.5 | convolution fusion | flops 806092800 | bytes 4194320 | tf_op jit(solution)/shard_map/bij,bjw->biw/dot_general | solution.py:29
  33.4 1.3 copy.15
  34.8 0.0 reduce-scatter.4.cloned.1.call-update
  34.8 0.0 reduce-scatter.6.cloned.1.call-start
  34.9 37.6 %reduce-scatter.4.cloned.1.call-done = f32[128,256]{1,0:T(8,128)} async-done(((f32[1024,256]{1,0:T(8,128)}), f32[128,256]{1,0:T(8,128)}) %reduce-scatter.4.cloned.1.call-update) | async-done | bytes 131088 | tf_op jit(solution)/shard_map/reduce_scatter | solution.py:30
  72.4 1.0 multiply_reduce_fusion.2
  73.5 1.0 multiply_convert_fusion.3
  74.5 13.8 %all_gather.10 = bf16[512,256]{1,0:T(8,128)(2,1)S(1)} all-gather(bf16[128,256]{1,0:T(8,128)(2,1)S(1)} %multiply_convert_fusion.3), channel_id=1, replica_groups=mesh['src'=8,'dst'=4] {'dst'}, dimensions={0}, use_global_device_ids=true | all-gather | bytes 327680 | tf_op jit(solution)/shard_map/all_gather | solution.py:24
  88.3 2.0 gather_fusion.1
  90.4 5.4 %bitcast_reduce_fusion.1 = f32[8,128,256]{1,2,0:T(8,128)S(1)} fusion(f32[16,128,128]{2,1,0:T(8,128)S(1)} %copy-done, f32[16,128,256]{2,1,0:T(8,128)} %gather_fusion.1, pred[16]{0:T(512)(128)(4,1)S(1)} %compare_and_fusion), kind=kOutput, calls=%fused_computation.4 | convolution fusion | flops 806092800 | bytes 4194320 | tf_op jit(solution)/shard_map/bij,bjw->biw/dot_general | solution.py:29
  95.8 1.3 copy.17
  97.2 0.0 reduce-scatter.6.cloned.1.call-update
  97.2 0.0 reduce-scatter.8.cloned.1.call-start
  97.2 36.7 %reduce-scatter.6.cloned.1.call-done = f32[128,256]{1,0:T(8,128)} async-done(((f32[1024,256]{1,0:T(8,128)}), f32[128,256]{1,0:T(8,128)}) %reduce-scatter.6.cloned.1.call-update) | async-done | bytes 131088 | tf_op jit(solution)/shard_map/reduce_scatter | solution.py:30
  133.9 1.0 multiply_reduce_fusion.1
  134.9 1.0 multiply_convert_fusion.2
  135.9 14.1 %all_gather.11 = bf16[512,256]{1,0:T(8,128)(2,1)S(1)} all-gather(bf16[128,256]{1,0:T(8,128)(2,1)S(1)} %multiply_convert_fusion.2), channel_id=1, replica_groups=mesh['src'=8,'dst'=4] {'dst'}, dimensions={0}, use_global_device_ids=true | all-gather | bytes 327680 | tf_op jit(solution)/shard_map/all_gather | solution.py:24
  150.0 2.0 gather_fusion.2
  152.1 5.4 %bitcast_reduce_fusion = f32[8,128,256]{1,2,0:T(8,128)S(1)} fusion(f32[16,128,128]{2,1,0:T(8,128)S(1)} %copy-done, f32[16,128,256]{2,1,0:T(8,128)} %gather_fusion.2, pred[16]{0:T(512)(128)(4,1)S(1)} %compare_and_fusion), kind=kOutput, calls=%fused_computation.3 | convolution fusion | flops 806092800 | bytes 4194320 | tf_op jit(solution)/shard_map/bij,bjw->biw/dot_general | solution.py:29
  157.5 1.3 copy.19
  158.8 0.0 reduce-scatter.8.cloned.1.call-update
  158.9 36.6 %reduce-scatter.8.cloned.1.call-done = f32[128,256]{1,0:T(8,128)} async-done(((f32[1024,256]{1,0:T(8,128)}), f32[128,256]{1,0:T(8,128)}) %reduce-scatter.8.cloned.1.call-update) | async-done | bytes 131088 | tf_op jit(solution)/shard_map/reduce_scatter | solution.py:30
  195.5 1.0 multiply_reduce_fusion
  196.5 1.0 fusion.19
  197.5 0.7 pad_maximum_fusion
  (14 shorter events, 0.2 us)
Async XLA Ops:
  7.2 20.8 %copy-start = (f32[16,128,128]{2,1,0:T(8,128)S(1)}, f32[16,128,128]{2,1,0:T(8,128)}, u32[]{:S(2)}) copy-start(f32[16,128,128]{2,1,0:T(8,128)} %param.11) | copy-start | bytes 3145732
  7.2 65.3 %reduce-scatter.4.cloned.1.call-start = ((), (), s32[]{:S(2)}) async-start(), calls=%async_computation.3 | async-start | bytes 1179648 | tf_op jit(solution)/shard_map/reduce_scatter | solution.py:30
  10.2 17.7 %copy-start.2 = (bf16[128,256]{1,0:T(8,128)(2,1)}, bf16[128,256]{1,0:T(8,128)(2,1)S(1)}, u32[]{:S(2)}) copy-start(bf16[128,256]{1,0:T(8,128)(2,1)S(1)} %multiply_convert_fusion.4) | copy-start | bytes 196612
  33.4 39.0 %copy-start.1 = (bf16[3,128,256]{2,1,0:T(8,128)(2,1)S(1)}, bf16[3,128,256]{2,1,0:T(8,128)(2,1)}, u32[]{:S(2)}) copy-start(bf16[3,128,256]{2,1,0:T(8,128)(2,1)} %param.13) | copy-start | bytes 589828
  34.8 99.1 %reduce-scatter.6.cloned.1.call-start = ((), (), s32[]{:S(2)}) async-start(), calls=%async_computation.4 | async-start | bytes 1179648 | tf_op jit(solution)/shard_map/reduce_scatter | solution.py:30
  97.2 98.3 %reduce-scatter.8.cloned.1.call-start = ((), (), s32[]{:S(2)}) async-start(), calls=%async_computation.5 | async-start | bytes 1179648 | tf_op jit(solution)/shard_map/reduce_scatter | solution.py:30
Sparse Core Ops, SparseCore 0:
  34.9 37.4 reduce-scatter.3
  97.3 36.5 reduce-scatter.5
  159.0 36.4 reduce-scatter.7
where the time goes:
time: 205 us
  waiting for transfers between devices  111 us (54%)
  blocking collectives  43.6 us (21%)
  matrix products  17.8 us (9%)
  between operations  13.9 us (7%)
  local copies, waits for them, and re-layouts  10.1 us (5%)
  other arithmetic  8.34 us (4%)
    reduce_scatter x3, waiting for transfers between devices, shards(): lax.psum_scatter(prods.reshape(own_rows * lax.axis_size('src') // block_s...  111 us
    all_gather x3, blocking collectives, shards(): group = lax.all_gather(feats, 'dst', axis=0, tiled=True)  43.6 us
    dot_general x3, matrix products, shards(): jnp.einsum('bij,bjw->biw', block_weights, fetched, precision=lax.Precisio...  16.3 us
    gather x3, local copies, waits for them, and re-layouts, shards(): fetched = jnp.take(col_blocks, block_cols, axis=0)  6.1 us
  transfers between devices with their start and end apart: 3, of which 3 were waited for; matrix products, arithmetic and copies ran while one was open for 0% of the time, Pallas kernels for 0%

commit v1 on v0

--- a/solution.py
+++ b/solution.py
@@ -4,6 +4,24 @@
 from jax.sharding import PartitionSpec as P
 
 HOPS = 3
+
+
+def collect(array, axis, dim):
+    ways, here, step = (lax.axis_size(axis), lax.axis_index(axis), array.shape[dim])
+    shape = [n * ways if d == dim else n for d, n in enumerate(array.shape)]
+    full = lax.dynamic_update_slice_in_dim(
+        jnp.zeros(shape, array.dtype), array, here * step, axis=dim
+    )
+    going_up = going_down = array
+    for far in range(1, ways // 2 + 1):
+        going_up = lax.ppermute(going_up, axis, [(d, (d + 1) % ways) for d in range(ways)])
+        full = lax.dynamic_update_slice_in_dim(full, going_up, (here - far) % ways * step, axis=dim)
+        if 2 * far < ways:
+            going_down = lax.ppermute(going_down, axis, [(d, (d - 1) % ways) for d in range(ways)])
+            full = lax.dynamic_update_slice_in_dim(
+                full, going_down, (here + far) % ways * step, axis=dim
+            )
+    return full
 
 
 def normalize_rows(z):
@@ -21,7 +39,7 @@
     feats = encoded
     kept = []
     for step in range(HOPS):
-        group = lax.all_gather(feats, "dst", axis=0, tiled=True)
+        group = collect(feats, "dst", 0)
         col_count = group.shape[0] // block_side
         half = col_count // 2
         col_blocks = group.astype(jnp.float32).reshape(col_count, block_side, width)

time: 205 us -> 190 us (0.927)
  blocking collectives: 43.6 us -> 0 us
  waiting for transfers between devices: 111 us -> 127 us
  starting transfers between devices: 0.12 us -> 13.1 us
    all_gather x3 -> x0, blocking collectives: 43.6 us -> none  [shards(): group = lax.all_gather(feats, 'dst', axis=0, tiled=True)]
    ppermute x0 -> x9, waiting for transfers between devices: none -> 25.9 us  [the longest x6 25.3 us: collect(): lax.ppermute(going_up, axis, [(d, (d + 1) % ways) for d in range(ways)])]
    ppermute x0 -> x9, starting transfers between devices: none -> 13 us  [the longest x3 6.78 us: collect(): lax.ppermute(going_down, axis, [(d, (d - 1) % ways) for d in range(ways)])]
    reduce_scatter x3, waiting for transfers between devices: 111 us -> 101 us  [shards(): lax.psum_scatter(prods.reshape(own_rows * lax.axis_size('src') // block_s...]
    convert_element_type x3 -> x0, other arithmetic: 2.09 us -> none  [normalize_rows(): (z * lax.rsqrt(jnp.mean(z * z, axis=-1, keepdims=True) + 1e-06)).astype(j...]
    dynamic_update_slice x0 -> x3, other arithmetic: none -> 2.07 us  [collect(): lax.dynamic_update_slice_in_dim(jnp.zeros(shape, array.dtype), array, her...]
  transfers between devices with their start and end apart: 3 -> 12, of which waited for: 3 -> 10; matrix products, arithmetic and copies ran while one was open for 0% -> 0% of each run, Pallas kernels for 0% -> 0%
where the time goes in v1:
time: 190 us; the launch traced here: 189 us
  waiting for transfers between devices  127 us (67%)
  matrix products  17.9 us (9%)
  between operations  14 us (7%)
  starting transfers between devices  13.1 us (7%)
  local copies, waits for them, and re-layouts  10.3 us (5%)
  other arithmetic  6.94 us (4%)
    reduce_scatter x3, waiting for transfers between devices, shards(): lax.psum_scatter(prods.reshape(own_rows * lax.axis_size('src') // block_s...  101 us
    ppermute x6, waiting for transfers between devices, collect(): lax.ppermute(going_up, axis, [(d, (d + 1) % ways) for d in range(ways)])  25.3 us
    dot_general x3, matrix products, shards(): jnp.einsum('bij,bjw->biw', block_weights, fetched, precision=lax.Precisio...  16.3 us
    ppermute x3, starting transfers between devices, collect(): lax.ppermute(going_down, axis, [(d, (d - 1) % ways) for d in range(ways)])  6.78 us
    ppermute x6, starting transfers between devices, collect(): lax.ppermute(going_up, axis, [(d, (d + 1) % ways) for d in range(ways)])  6.17 us
    gather x3, local copies, waits for them, and re-layouts, shards(): fetched = jnp.take(col_blocks, block_cols, axis=0)  6.1 us
    reduce_sum x3, local copies, waits for them, and re-layouts, shards(): mine = lax.psum_scatter(prods.reshape(own_rows * lax.axis_size('src') //...  3.98 us
  transfers between devices with their start and end apart: 12, of which 10 were waited for; matrix products, arithmetic and copies ran while one was open for 0% of the time, Pallas kernels for 0%

profile of v1, /device:TPU:0, one launch (start us, length us, event | category | flops | bytes accessed | tf_op | source)
XLA Modules:
  0.0 189.5 jit_solution(11668871444719183923)
XLA Ops:
  7.2 1.6 multiply_reduce_fusion.3
  9.0 3.1 %collective-permute-start = (bf16[128,256]{1,0:T(8,128)(2,1)S(1)}, bf16[128,256]{1,0:T(8,128)(2,1)S(1)}, u32[]{:S(2)}, u32[]{:S(2)}) collective-permute-start(bf16[128,256]{1,0:T(8,128)(2,1)S(1)} %get-tuple-element.8), channel_id=1, source_target_pairs={{0,1},{1,2},{2,3},{3,0},{4,5},{5,6},{6,7},{7,4},{8,9},{9,10},{10,1... | collective-permute-start | bytes 196616 | tf_op jit(solution)/shard_map/ppermute | solution.py:17
  12.1 2.1 %collective-permute-start.1 = (bf16[128,256]{1,0:T(8,128)(2,1)S(1)}, bf16[128,256]{1,0:T(8,128)(2,1)S(1)}, u32[]{:S(2)}, u32[]{:S(2)}) collective-permute-start(bf16[128,256]{1,0:T(8,128)(2,1)S(1)} %get-tuple-element.8), channel_id=1, source_target_pairs={{0,3},{1,0},{2,1},{3,2},{4,7},{5,4},{6,5},{7,6},{8,11},{9,8},{10,9... | collective-permute-start | bytes 196616 | tf_op jit(solution)/shard_map/ppermute | solution.py:20
  14.2 2.2 %collective-permute-done = bf16[128,256]{1,0:T(8,128)(2,1)S(1)} collective-permute-done((bf16[128,256]{1,0:T(8,128)(2,1)S(1)}, bf16[128,256]{1,0:T(8,128)(2,1)S(1)}, u32[]{:S(2)}, u32[]{:S(2)}) %collective-permute-start) | collective-permute-done | bytes 65568 | tf_op jit(solution)/shard_map/ppermute | solution.py:17
  17.0 5.5 %collective-permute-done.2 = bf16[128,256]{1,0:T(8,128)(2,1)S(1)} collective-permute-done((bf16[128,256]{1,0:T(8,128)(2,1)S(1)}, bf16[128,256]{1,0:T(8,128)(2,1)S(1)}, u32[]{:S(2)}, u32[]{:S(2)}) %collective-permute-start.2) | collective-permute-done | bytes 65568 | tf_op jit(solution)/shard_map/ppermute | solution.py:17
  22.6 2.0 %gather_fusion = f32[16,128,256]{2,1,0:T(8,128)} fusion(f32[4,128,256]{2,1,0:T(8,128)S(1)} %convert.6, s32[1024]{0:T(1024)S(1)} %pad_clamp_fusion), kind=kCustom, calls=%fused_computation.clone | custom fusion | bytes 4194368 | tf_op jit(solution)/shard_map/jit(_take)/gather | solution.py:46
  24.6 5.4 %bitcast_reduce_fusion.2 = f32[8,128,256]{1,2,0:T(8,128)S(1)} fusion(f32[16,128,128]{2,1,0:T(8,128)S(1)} %copy-done, f32[16,128,256]{2,1,0:T(8,128)} %gather_fusion, pred[16]{0:T(512)(128)(4,1)S(1)} %compare_and_fusion), kind=kOutput, calls=%fused_computation.5 | convolution fusion | flops 806092800 | bytes 4194320 | tf_op jit(solution)/shard_map/bij,bjw->biw/dot_general | solution.py:47
  30.1 1.3 copy.15
  31.5 34.7 %reduce-scatter.4.cloned.1.call-done = f32[128,256]{1,0:T(8,128)} async-done(((f32[1024,256]{1,0:T(8,128)}), f32[128,256]{1,0:T(8,128)}) %reduce-scatter.4.cloned.1.call-update) | async-done | bytes 131088 | tf_op jit(solution)/shard_map/reduce_scatter | solution.py:48
  66.2 1.0 multiply_reduce_fusion.2
  67.2 1.0 constant_dynamic-update-slice_fusion.7
  68.2 1.5 collective-permute-start.3
  69.8 2.3 %collective-permute-start.4 = (bf16[128,256]{1,0:T(8,128)(2,1)S(1)}, bf16[128,256]{1,0:T(8,128)(2,1)S(1)}, u32[]{:S(2)}, u32[]{:S(2)}) collective-permute-start(bf16[128,256]{1,0:T(8,128)(2,1)S(1)} %get-tuple-element.6), channel_id=1, source_target_pairs={{0,3},{1,0},{2,1},{3,2},{4,7},{5,4},{6,5},{7,6},{8,11},{9,8},{10,9... | collective-permute-start | bytes 196616 | tf_op jit(solution)/shard_map/ppermute | solution.py:20
  72.1 2.8 %collective-permute-done.3 = bf16[128,256]{1,0:T(8,128)(2,1)S(1)} collective-permute-done((bf16[128,256]{1,0:T(8,128)(2,1)S(1)}, bf16[128,256]{1,0:T(8,128)(2,1)S(1)}, u32[]{:S(2)}, u32[]{:S(2)}) %collective-permute-start.3) | collective-permute-done | bytes 65568 | tf_op jit(solution)/shard_map/ppermute | solution.py:17
  75.0 6.0 %collective-permute-done.5 = bf16[128,256]{1,0:T(8,128)(2,1)S(1)} collective-permute-done((bf16[128,256]{1,0:T(8,128)(2,1)S(1)}, bf16[128,256]{1,0:T(8,128)(2,1)S(1)}, u32[]{:S(2)}, u32[]{:S(2)}) %collective-permute-start.5) | collective-permute-done | bytes 65568 | tf_op jit(solution)/shard_map/ppermute | solution.py:17
  81.0 2.0 %gather_fusion.1 = f32[16,128,256]{2,1,0:T(8,128)} fusion(f32[4,128,256]{2,1,0:T(8,128)S(1)} %convert.8, s32[1024]{0:T(1024)S(1)} %pad_clamp_fusion), kind=kCustom, calls=%fused_computation.1.clone | custom fusion | bytes 4194368 | tf_op jit(solution)/shard_map/jit(_take)/gather | solution.py:46
  83.1 5.4 %bitcast_reduce_fusion.1 = f32[8,128,256]{1,2,0:T(8,128)S(1)} fusion(f32[16,128,128]{2,1,0:T(8,128)S(1)} %copy-done, f32[16,128,256]{2,1,0:T(8,128)} %gather_fusion.1, pred[16]{0:T(512)(128)(4,1)S(1)} %compare_and_fusion), kind=kOutput, calls=%fused_computation.4 | convolution fusion | flops 806092800 | bytes 4194320 | tf_op jit(solution)/shard_map/bij,bjw->biw/dot_general | solution.py:47
  88.5 1.3 copy.17
  89.9 33.3 %reduce-scatter.6.cloned.1.call-done = f32[128,256]{1,0:T(8,128)} async-done(((f32[1024,256]{1,0:T(8,128)}), f32[128,256]{1,0:T(8,128)}) %reduce-scatter.6.cloned.1.call-update) | async-done | bytes 131088 | tf_op jit(solution)/shard_map/reduce_scatter | solution.py:48
  123.3 1.0 multiply_reduce_fusion.1
  124.3 1.0 constant_dynamic-update-slice_fusion.3
  125.3 1.5 collective-permute-start.6
  126.8 2.3 %collective-permute-start.7 = (bf16[128,256]{1,0:T(8,128)(2,1)S(1)}, bf16[128,256]{1,0:T(8,128)(2,1)S(1)}, u32[]{:S(2)}, u32[]{:S(2)}) collective-permute-start(bf16[128,256]{1,0:T(8,128)(2,1)S(1)} %get-tuple-element.4), channel_id=1, source_target_pairs={{0,3},{1,0},{2,1},{3,2},{4,7},{5,4},{6,5},{7,6},{8,11},{9,8},{10,9... | collective-permute-start | bytes 196616 | tf_op jit(solution)/shard_map/ppermute | solution.py:20
  129.2 2.8 %collective-permute-done.6 = bf16[128,256]{1,0:T(8,128)(2,1)S(1)} collective-permute-done((bf16[128,256]{1,0:T(8,128)(2,1)S(1)}, bf16[128,256]{1,0:T(8,128)(2,1)S(1)}, u32[]{:S(2)}, u32[]{:S(2)}) %collective-permute-start.6) | collective-permute-done | bytes 65568 | tf_op jit(solution)/shard_map/ppermute | solution.py:17
  132.0 6.0 %collective-permute-done.8 = bf16[128,256]{1,0:T(8,128)(2,1)S(1)} collective-permute-done((bf16[128,256]{1,0:T(8,128)(2,1)S(1)}, bf16[128,256]{1,0:T(8,128)(2,1)S(1)}, u32[]{:S(2)}, u32[]{:S(2)}) %collective-permute-start.8) | collective-permute-done | bytes 65568 | tf_op jit(solution)/shard_map/ppermute | solution.py:17
  138.1 2.0 %gather_fusion.2 = f32[16,128,256]{2,1,0:T(8,128)} fusion(f32[4,128,256]{2,1,0:T(8,128)S(1)} %convert.10, s32[1024]{0:T(1024)S(1)} %pad_clamp_fusion), kind=kCustom, calls=%fused_computation.2.clone | custom fusion | bytes 4194368 | tf_op jit(solution)/shard_map/jit(_take)/gather | solution.py:46
  140.1 5.4 %bitcast_reduce_fusion = f32[8,128,256]{1,2,0:T(8,128)S(1)} fusion(f32[16,128,128]{2,1,0:T(8,128)S(1)} %copy-done, f32[16,128,256]{2,1,0:T(8,128)} %gather_fusion.2, pred[16]{0:T(512)(128)(4,1)S(1)} %compare_and_fusion), kind=kOutput, calls=%fused_computation.3 | convolution fusion | flops 806092800 | bytes 4194320 | tf_op jit(solution)/shard_map/bij,bjw->biw/dot_general | solution.py:47
  145.6 1.3 copy.19
  146.9 33.3 %reduce-scatter.8.cloned.1.call-done = f32[128,256]{1,0:T(8,128)} async-done(((f32[1024,256]{1,0:T(8,128)}), f32[128,256]{1,0:T(8,128)}) %reduce-scatter.8.cloned.1.call-update) | async-done | bytes 131088 | tf_op jit(solution)/shard_map/reduce_scatter | solution.py:48
  180.2 1.0 multiply_reduce_fusion
  181.3 1.0 fusion.19
  182.3 0.7 pad_maximum_fusion
  (43 shorter events, 1.2 us)
Async XLA Ops:
  7.2 17.4 %copy-start = (f32[16,128,128]{2,1,0:T(8,128)S(1)}, f32[16,128,128]{2,1,0:T(8,128)}, u32[]{:S(2)}) copy-start(f32[16,128,128]{2,1,0:T(8,128)} %param.11) | copy-start | bytes 3145732
  7.2 7.0 %copy-start.3 = (s32[16]{0:T(128)S(1)}, s32[16]{0:T(128)}, u32[]{:S(2)}) copy-start(s32[16]{0:T(128)} %param.12) | copy-start | bytes 196
  7.2 59.0 %reduce-scatter.4.cloned.1.call-start = ((), (), s32[]{:S(2)}) async-start(), calls=%async_computation.3 | async-start | bytes 1179648 | tf_op jit(solution)/shard_map/reduce_scatter | solution.py:48
  8.9 15.6 %copy-start.2 = (bf16[128,256]{1,0:T(8,128)(2,1)}, bf16[128,256]{1,0:T(8,128)(2,1)S(1)}, u32[]{:S(2)}) copy-start(bf16[128,256]{1,0:T(8,128)(2,1)S(1)} %get-tuple-element.8) | copy-start | bytes 196612
  9.0 7.5 %collective-permute-start = (bf16[128,256]{1,0:T(8,128)(2,1)S(1)}, bf16[128,256]{1,0:T(8,128)(2,1)S(1)}, u32[]{:S(2)}, u32[]{:S(2)}) collective-permute-start(bf16[128,256]{1,0:T(8,128)(2,1)S(1)} %get-tuple-element.8), channel_id=1, source_target_pairs={{0,1},{1,2},{2,3},{3,0},{4,5},{5,6},{6,7},{7,4},{8,9},{9,10},{10,1... | collective-permute-start | bytes 196616 | tf_op jit(solution)/shard_map/ppermute | solution.py:17
  12.1 5.0 %collective-permute-start.1 = (bf16[128,256]{1,0:T(8,128)(2,1)S(1)}, bf16[128,256]{1,0:T(8,128)(2,1)S(1)}, u32[]{:S(2)}, u32[]{:S(2)}) collective-permute-start(bf16[128,256]{1,0:T(8,128)(2,1)S(1)} %get-tuple-element.8), channel_id=1, source_target_pairs={{0,3},{1,0},{2,1},{3,2},{4,7},{5,4},{6,5},{7,6},{8,11},{9,8},{10,9... | collective-permute-start | bytes 196616 | tf_op jit(solution)/shard_map/ppermute | solution.py:20
  16.4 6.1 %collective-permute-start.2 = (bf16[128,256]{1,0:T(8,128)(2,1)S(1)}, bf16[128,256]{1,0:T(8,128)(2,1)S(1)}, u32[]{:S(2)}, u32[]{:S(2)}) collective-permute-start(bf16[128,256]{1,0:T(8,128)(2,1)S(1)} %collective-permute-done), channel_id=1, source_target_pairs={{0,1},{1,2},{2,3},{3,0},{4,5},{5,6},{6,7},{7,4},{8,9},{9,10},{10,1... | collective-permute-start | bytes 196616 | tf_op jit(solution)/shard_map/ppermute | solution.py:17
  30.0 36.1 %copy-start.1 = (bf16[3,128,256]{2,1,0:T(8,128)(2,1)S(1)}, bf16[3,128,256]{2,1,0:T(8,128)(2,1)}, u32[]{:S(2)}) copy-start(bf16[3,128,256]{2,1,0:T(8,128)(2,1)} %param.13) | copy-start | bytes 589828
  31.4 91.8 %reduce-scatter.6.cloned.1.call-start = ((), (), s32[]{:S(2)}) async-start(), calls=%async_computation.4 | async-start | bytes 1179648 | tf_op jit(solution)/shard_map/reduce_scatter | solution.py:48
  68.2 6.7 %collective-permute-start.3 = (bf16[128,256]{1,0:T(8,128)(2,1)S(1)}, bf16[128,256]{1,0:T(8,128)(2,1)S(1)}, u32[]{:S(2)}, u32[]{:S(2)}) collective-permute-start(bf16[128,256]{1,0:T(8,128)(2,1)S(1)} %get-tuple-element.6), channel_id=1, source_target_pairs={{0,1},{1,2},{2,3},{3,0},{4,5},{5,6},{6,7},{7,4},{8,9},{9,10},{10,1... | collective-permute-start | bytes 196616 | tf_op jit(solution)/shard_map/ppermute | solution.py:17
  69.8 5.2 %collective-permute-start.4 = (bf16[128,256]{1,0:T(8,128)(2,1)S(1)}, bf16[128,256]{1,0:T(8,128)(2,1)S(1)}, u32[]{:S(2)}, u32[]{:S(2)}) collective-permute-start(bf16[128,256]{1,0:T(8,128)(2,1)S(1)} %get-tuple-element.6), channel_id=1, source_target_pairs={{0,3},{1,0},{2,1},{3,2},{4,7},{5,4},{6,5},{7,6},{8,11},{9,8},{10,9... | collective-permute-start | bytes 196616 | tf_op jit(solution)/shard_map/ppermute | solution.py:20
  74.9 6.1 %collective-permute-start.5 = (bf16[128,256]{1,0:T(8,128)(2,1)S(1)}, bf16[128,256]{1,0:T(8,128)(2,1)S(1)}, u32[]{:S(2)}, u32[]{:S(2)}) collective-permute-start(bf16[128,256]{1,0:T(8,128)(2,1)S(1)} %collective-permute-done.3), channel_id=1, source_target_pairs={{0,1},{1,2},{2,3},{3,0},{4,5},{5,6},{6,7},{7,4},{8,9},{9,10},{10,1... | collective-permute-start | bytes 196616 | tf_op jit(solution)/shard_map/ppermute | solution.py:17
  89.9 90.4 %reduce-scatter.8.cloned.1.call-start = ((), (), s32[]{:S(2)}) async-start(), calls=%async_computation.5 | async-start | bytes 1179648 | tf_op jit(solution)/shard_map/reduce_scatter | solution.py:48
  125.3 6.7 %collective-permute-start.6 = (bf16[128,256]{1,0:T(8,128)(2,1)S(1)}, bf16[128,256]{1,0:T(8,128)(2,1)S(1)}, u32[]{:S(2)}, u32[]{:S(2)}) collective-permute-start(bf16[128,256]{1,0:T(8,128)(2,1)S(1)} %get-tuple-element.4), channel_id=1, source_target_pairs={{0,1},{1,2},{2,3},{3,0},{4,5},{5,6},{6,7},{7,4},{8,9},{9,10},{10,1... | collective-permute-start | bytes 196616 | tf_op jit(solution)/shard_map/ppermute | solution.py:17
  126.8 5.1 %collective-permute-start.7 = (bf16[128,256]{1,0:T(8,128)(2,1)S(1)}, bf16[128,256]{1,0:T(8,128)(2,1)S(1)}, u32[]{:S(2)}, u32[]{:S(2)}) collective-permute-start(bf16[128,256]{1,0:T(8,128)(2,1)S(1)} %get-tuple-element.4), channel_id=1, source_target_pairs={{0,3},{1,0},{2,1},{3,2},{4,7},{5,4},{6,5},{7,6},{8,11},{9,8},{10,9... | collective-permute-start | bytes 196616 | tf_op jit(solution)/shard_map/ppermute | solution.py:20
  132.0 6.1 %collective-permute-start.8 = (bf16[128,256]{1,0:T(8,128)(2,1)S(1)}, bf16[128,256]{1,0:T(8,128)(2,1)S(1)}, u32[]{:S(2)}, u32[]{:S(2)}) collective-permute-start(bf16[128,256]{1,0:T(8,128)(2,1)S(1)} %collective-permute-done.6), channel_id=1, source_target_pairs={{0,1},{1,2},{2,3},{3,0},{4,5},{5,6},{6,7},{7,4},{8,9},{9,10},{10,1... | collective-permute-start | bytes 196616 | tf_op jit(solution)/shard_map/ppermute | solution.py:17
Sparse Core Ops, SparseCore 0:
  31.5 34.6 reduce-scatter.3
  90.0 33.2 reduce-scatter.5
  147.0 33.1 reduce-scatter.7
